TPU v7x, 512 devices: a whole 4x4x16 slice. The times are simulated.
512 devices in a mesh: dom: 64 (over z, y), rep: 8 (over x, core).
Axes of the slice: x: 4, y: 4, z: 16, core: 2. Of those that a mesh axis runs over, the one named last changes fastest.
Arguments:
- feats: bfloat16 [65536, 128], P(('dom', 'rep')), may hold values from -6 to 6
- weight: bfloat16 [128, 128], replicated, may hold values from -0.5 to 0.5
- bias: float32 [128], replicated, may hold values from -3 to 3
- tiles: bfloat16 [512, 5, 28, 128, 128], P(('dom', 'rep')), may hold values from -0.0625 to 0.0625
- tile_cols: int32 [512, 5, 28], P(('dom', 'rep')), may hold values from 0 to 7
- tile_count: int32 [512, 5], P(('dom', 'rep')), may hold values from 2 to 28, as said below
- cotangent: bfloat16 [65536, 128], P(('dom', 'rep')), may hold values from -6 to 6
Outputs:
- hidden: bfloat16 [65536, 128], P(('dom', 'rep'))
- grad_weight: float32 [128, 128], replicated
- grad_bias: float32 [128], replicated
- grad_feats: bfloat16 [65536, 128], P(('dom', 'rep'))
Inputs may be any that keep to these rules, and one draw needn't show every extreme that they name: `tile_count`: every list has at least two live tiles; the nodes of some device have 28 live tiles in every list, and those of most devices far fewer.
All inputs are finite; a program needn't handle non-finite values.
Results may differ from a plain program's by a relative error of at most 0.0062.
Values may be sent and summed in bfloat16 or wider, within the bound.
A program may use at most 64 MiB of HBM per device.

v0:
```python
import jax
import jax.numpy as jnp
from jax import lax
from jax.sharding import PartitionSpec as P


def swapped(value, axis, bit):
    mask = 2**bit
    pairs = [(source, source ^ mask) for source in range(lax.axis_size(axis))]
    return lax.ppermute(value, axis, pairs)


def gelu_tanh(values):
    return jax.nn.gelu(values, approximate=True)


def add_slot(summed, panel, slot, tiles, tile_cols, live_mask):
    tgt_blocks, slot_count, max_tiles, block, unused = tiles.shape
    width = panel.shape[1]
    panel_blocks = panel.shape[0] // block
    source = panel.reshape(panel_blocks, block, width)
    columns = tile_cols[:, slot]
    slot_tiles = tiles[:, slot]
    fetched = source[columns]
    fetched = jnp.where(live_mask[:, slot][:, :, None, None], fetched, jnp.zeros((), jnp.bfloat16))
    return summed + jnp.einsum(
        "tmij,tmjh->tih", slot_tiles, fetched, preferred_element_type=jnp.float32
    )


def partial_panel(slot, tiles, tile_cols, live_mask, grad_rows_b, panel_blocks):
    tgt_blocks, slot_count, max_tiles, block, unused = tiles.shape
    width = grad_rows_b.shape[2]
    masked = jnp.where(
        live_mask[:, slot][:, :, None, None], tiles[:, slot], jnp.zeros((), jnp.bfloat16)
    )
    contrib = jnp.einsum("tmij,tih->tmjh", masked, grad_rows_b, preferred_element_type=jnp.float32)
    targets = tile_cols[:, slot].reshape(tgt_blocks * max_tiles)
    placed = jnp.zeros((panel_blocks, block, width), jnp.float32)
    placed = placed.at[targets].add(contrib.reshape(tgt_blocks * max_tiles, block, width))
    return placed.reshape(panel_blocks * block, width)


def body(feats, weight, bias, tiles, tile_cols, tile_count, cotangent):
    dom_size = lax.axis_size("dom")
    rep_size = lax.axis_size("rep")
    top_bit = dom_size.bit_length() - 1
    tgt_blocks, slot_count, max_tiles, block, unused = tiles.shape
    width = weight.shape[1]
    panel_blocks = rep_size * tgt_blocks
    live_mask = jnp.arange(max_tiles)[None, None, :] < tile_count[:, :, None]
    projected = jnp.dot(feats, weight, preferred_element_type=jnp.float32).astype(jnp.bfloat16)
    own_rows = lax.all_gather(projected, "rep", axis=0, tiled=True)
    summed = jnp.zeros((tgt_blocks, block, width), jnp.float32)
    summed = add_slot(summed, own_rows, 0, tiles, tile_cols, live_mask)
    for round_index in range(1, slot_count):
        bit_number = top_bit - round_index
        partner_rows = swapped(own_rows, "dom", bit_number)
        summed = add_slot(summed, partner_rows, round_index, tiles, tile_cols, live_mask)
    preact = summed.reshape(tgt_blocks * block, width) + bias
    hidden_f, pullback = jax.vjp(gelu_tanh, preact)
    hidden = hidden_f.astype(jnp.bfloat16)
    grad_pre = pullback(cotangent.astype(jnp.float32))[0]
    grad_rows_b = grad_pre.astype(jnp.bfloat16).reshape(tgt_blocks, block, width)
    grad_panel = partial_panel(0, tiles, tile_cols, live_mask, grad_rows_b, panel_blocks)
    for round_index in range(1, slot_count):
        outgoing = partial_panel(
            round_index, tiles, tile_cols, live_mask, grad_rows_b, panel_blocks
        )
        grad_panel = grad_panel + swapped(outgoing, "dom", top_bit - round_index)
    grad_proj = lax.psum_scatter(grad_panel, "rep", scatter_dimension=0, tiled=True).astype(
        jnp.bfloat16
    )
    weight_local = lax.dot_general(
        feats, grad_proj, (((0,), (0,)), ((), ())), preferred_element_type=jnp.float32
    )
    bias_local = jnp.sum(grad_pre, axis=0)
    grad_weight, grad_bias = lax.psum((weight_local, bias_local), ("dom", "rep"))
    grad_feats = lax.dot_general(
        grad_proj, weight, (((1,), (1,)), ((), ())), preferred_element_type=jnp.float32
    ).astype(jnp.bfloat16)
    return (hidden, grad_weight, grad_bias, grad_feats)


def solution(mesh):
    return jax.shard_map(
        body,
        mesh=mesh,
        in_specs=(
            P(("dom", "rep"), None),
            P(),
            P(),
            P(("dom", "rep"), None, None, None, None),
            P(("dom", "rep"), None, None),
            P(("dom", "rep"), None),
            P(("dom", "rep"), None),
        ),
        out_specs=(P(("dom", "rep"), None), P(), P(), P(("dom", "rep"), None)),
        check_vma=False,
    )
```

profile of v0, /device:TPU:1, one launch (start us, length us, event | category | flops | bytes accessed | tf_op | source)
XLA Modules:
  0.0 770.6 jit_solution(12770402989602264046)
XLA Ops:
  8.8 19.5 %all_gather.3 = bf16[1024,128]{1,0:T(8,128)(2,1)S(1)} all-gather(bf16[128,128]{1,0:T(8,128)(2,1)S(1)} %convolution_convert_fusion.1), channel_id=1, replica_groups=mesh['dom'=64,'rep'=8] {'rep'}, dimensions={0}, use_global_device_ids=true | all-gather | bytes 294912 | tf_op jit(solution)/shard_map/all_gather | solution.py:53
  28.3 1.9 collective-permute-start.3
  30.2 1.9 collective-permute-start.2
  32.2 8.4 %collective-permute-start.1 = (bf16[1024,128]{1,0:T(8,128)(2,1)S(1)}, bf16[1024,128]{1,0:T(8,128)(2,1)S(1)}, u32[]{:S(2)}, u32[]{:S(2)}) collective-permute-start(bf16[1024,128]{1,0:T(8,128)(2,1)S(1)} %all_gather.3), channel_id=1, source_target_pairs={{0,128},{8,136},{16,144},{24,152},{32,160},{40,168},{48,176},{56,1... | collective-permute-start | bytes 786440 | tf_op jit(solution)/shard_map/ppermute | solution.py:10
  40.6 7.9 %collective-permute-start = (bf16[1024,128]{1,0:T(8,128)(2,1)S(1)}, bf16[1024,128]{1,0:T(8,128)(2,1)S(1)}, u32[]{:S(2)}, u32[]{:S(2)}) collective-permute-start(bf16[1024,128]{1,0:T(8,128)(2,1)S(1)} %all_gather.3), channel_id=1, source_target_pairs={{0,256},{8,264},{16,272},{24,280},{32,288},{40,296},{48,304},{56,3... | collective-permute-start | bytes 786440 | tf_op jit(solution)/shard_map/ppermute | solution.py:10
  51.5 1.6 convolution_bitcast_fusion.4
  53.9 1.6 convolution_bitcast_fusion
  55.6 8.0 %collective-permute-done.2 = bf16[1024,128]{1,0:T(8,128)(2,1)S(1)} collective-permute-done((bf16[1024,128]{1,0:T(8,128)(2,1)S(1)}, bf16[1024,128]{1,0:T(8,128)(2,1)S(1)}, u32[]{:S(2)}, u32[]{:S(2)}) %collective-permute-start.2) | collective-permute-done | bytes 262176 | tf_op jit(solution)/shard_map/ppermute | solution.py:10
  64.3 1.6 convolution_bitcast_fusion.1
  66.0 19.9 %collective-permute-done.1 = bf16[1024,128]{1,0:T(8,128)(2,1)S(1)} collective-permute-done((bf16[1024,128]{1,0:T(8,128)(2,1)S(1)}, bf16[1024,128]{1,0:T(8,128)(2,1)S(1)}, u32[]{:S(2)}, u32[]{:S(2)}) %collective-permute-start.1) | collective-permute-done | bytes 262176 | tf_op jit(solution)/shard_map/ppermute | solution.py:10
  86.7 1.6 convolution_bitcast_fusion.2
  89.1 2.3 fusion.100
  91.4 3.2 fusion.12
  94.6 3.2 fusion.10
  97.8 2.0 fusion.8
  99.8 3.2 fusion.6
  103.0 4.6 scatter_fusion.1
  107.6 11.3 %collective-permute-start.4 = (f32[1024,128]{1,0:T(8,128)S(1)}, f32[1024,128]{1,0:T(8,128)}, u32[]{:S(2)}, u32[]{:S(2)}) collective-permute-start(f32[1024,128]{1,0:T(8,128)S(1)} %bitcast.141), channel_id=1, source_target_pairs={{0,256},{8,264},{16,272},{24,280},{32,288},{40,296},{48,304},{56,3... | collective-permute-start | bytes 1572872 | tf_op jit(solution)/shard_map/ppermute | solution.py:10
  118.9 4.6 scatter_fusion.2
  123.5 1.9 collective-permute-start.5
  125.5 2.6 scatter_fusion.3
  128.1 1.9 collective-permute-start.6
  130.1 4.6 scatter_fusion.4
  134.7 1.9 collective-permute-start.7
  136.6 3.2 fusion.14
  139.9 4.6 scatter_fusion
  144.5 8.1 %collective-permute-done.4 = f32[1024,128]{1,0:T(8,128)} collective-permute-done((f32[1024,128]{1,0:T(8,128)S(1)}, f32[1024,128]{1,0:T(8,128)}, u32[]{:S(2)}, u32[]{:S(2)}) %collective-permute-start.4) | collective-permute-done | bytes 524320 | tf_op jit(solution)/shard_map/ppermute | solution.py:10
  152.5 51.6 %collective-permute-done.5 = f32[1024,128]{1,0:T(8,128)} collective-permute-done((f32[1024,128]{1,0:T(8,128)S(1)}, f32[1024,128]{1,0:T(8,128)}, u32[]{:S(2)}, u32[]{:S(2)}) %collective-permute-start.5) | collective-permute-done | bytes 524320 | tf_op jit(solution)/shard_map/ppermute | solution.py:10
  204.2 2.3 fusion.53
  206.5 114.1 %psum.15 = f32[128]{0:T(128)} all-reduce(f32[128]{0:T(128)S(1)} %get-tuple-element.8), channel_id=1, replica_groups=mesh['dom'=64,'rep'=8] {'dom','rep'}, use_global_device_ids=true, to_apply=%region_8.9 | all-reduce | flops 128 | bytes 1024 | tf_op jit(solution)/shard_map/psum | solution.py:78
  320.7 1.7 convolution_bitcast_fusion.5
  324.0 438.2 %all-reduce.2.cloned.1.call-done = f32[128,128]{0,1:T(8,128)} async-done(((f32[128,128]{0,1:T(8,128)}), f32[128,128]{0,1:T(8,128)}) %all-reduce.2.cloned.1.call-update) | async-done | bytes 65552 | tf_op jit(solution)/shard_map/psum | solution.py:78
  (39 shorter events, 10.9 us)
Async XLA Ops:
  7.2 0.8 copy-start
  7.2 313.5 %reduce-scatter.2.cloned.1.call-start = ((), (), s32[]{:S(2)}) async-start(), calls=%async_computation.1 | async-start | bytes 589824 | tf_op jit(solution)/shard_map/reduce_scatter | solution.py:71
  28.3 24.9 %collective-permute-start.3 = (bf16[1024,128]{1,0:T(8,128)(2,1)S(1)}, bf16[1024,128]{1,0:T(8,128)(2,1)S(1)}, u32[]{:S(2)}, u32[]{:S(2)}) collective-permute-start(bf16[1024,128]{1,0:T(8,128)(2,1)S(1)} %all_gather.3), channel_id=1, source_target_pairs={{0,32},{8,40},{16,48},{24,56},{32,0},{40,8},{48,16},{56,24},{64,96... | collective-permute-start | bytes 786440 | tf_op jit(solution)/shard_map/ppermute | solution.py:10
  30.2 33.4 %collective-permute-start.2 = (bf16[1024,128]{1,0:T(8,128)(2,1)S(1)}, bf16[1024,128]{1,0:T(8,128)(2,1)S(1)}, u32[]{:S(2)}, u32[]{:S(2)}) collective-permute-start(bf16[1024,128]{1,0:T(8,128)(2,1)S(1)} %all_gather.3), channel_id=1, source_target_pairs={{0,64},{8,72},{16,80},{24,88},{32,96},{40,104},{48,112},{56,120},{... | collective-permute-start | bytes 786440 | tf_op jit(solution)/shard_map/ppermute | solution.py:10
  32.2 53.7 %collective-permute-start.1 = (bf16[1024,128]{1,0:T(8,128)(2,1)S(1)}, bf16[1024,128]{1,0:T(8,128)(2,1)S(1)}, u32[]{:S(2)}, u32[]{:S(2)}) collective-permute-start(bf16[1024,128]{1,0:T(8,128)(2,1)S(1)} %all_gather.3), channel_id=1, source_target_pairs={{0,128},{8,136},{16,144},{24,152},{32,160},{40,168},{48,176},{56,1... | collective-permute-start | bytes 786440 | tf_op jit(solution)/shard_map/ppermute | solution.py:10
  40.6 47.7 %collective-permute-start = (bf16[1024,128]{1,0:T(8,128)(2,1)S(1)}, bf16[1024,128]{1,0:T(8,128)(2,1)S(1)}, u32[]{:S(2)}, u32[]{:S(2)}) collective-permute-start(bf16[1024,128]{1,0:T(8,128)(2,1)S(1)} %all_gather.3), channel_id=1, source_target_pairs={{0,256},{8,264},{16,272},{24,280},{32,288},{40,296},{48,304},{56,3... | collective-permute-start | bytes 786440 | tf_op jit(solution)/shard_map/ppermute | solution.py:10
  86.6 2.4 copy-start.2
  86.6 2.4 copy-start.3
  107.6 44.9 %collective-permute-start.4 = (f32[1024,128]{1,0:T(8,128)S(1)}, f32[1024,128]{1,0:T(8,128)}, u32[]{:S(2)}, u32[]{:S(2)}) collective-permute-start(f32[1024,128]{1,0:T(8,128)S(1)} %bitcast.141), channel_id=1, source_target_pairs={{0,256},{8,264},{16,272},{24,280},{32,288},{40,296},{48,304},{56,3... | collective-permute-start | bytes 1572872 | tf_op jit(solution)/shard_map/ppermute | solution.py:10
  123.5 80.7 %collective-permute-start.5 = (f32[1024,128]{1,0:T(8,128)S(1)}, f32[1024,128]{1,0:T(8,128)}, u32[]{:S(2)}, u32[]{:S(2)}) collective-permute-start(f32[1024,128]{1,0:T(8,128)S(1)} %bitcast.142), channel_id=1, source_target_pairs={{0,128},{8,136},{16,144},{24,152},{32,160},{40,168},{48,176},{56,1... | collective-permute-start | bytes 1572872 | tf_op jit(solution)/shard_map/ppermute | solution.py:10
  128.1 76.1 %collective-permute-start.6 = (f32[1024,128]{1,0:T(8,128)S(1)}, f32[1024,128]{1,0:T(8,128)S(1)}, u32[]{:S(2)}, u32[]{:S(2)}) collective-permute-start(f32[1024,128]{1,0:T(8,128)S(1)} %bitcast.143), channel_id=1, source_target_pairs={{0,64},{8,72},{16,80},{24,88},{32,96},{40,104},{48,112},{56,120},{... | collective-permute-start | bytes 1572872 | tf_op jit(solution)/shard_map/ppermute | solution.py:10
  134.7 69.5 %collective-permute-start.7 = (f32[1024,128]{1,0:T(8,128)S(1)}, f32[1024,128]{1,0:T(8,128)}, u32[]{:S(2)}, u32[]{:S(2)}) collective-permute-start(f32[1024,128]{1,0:T(8,128)S(1)} %bitcast.144), channel_id=1, source_target_pairs={{0,32},{8,40},{16,48},{24,56},{32,0},{40,8},{48,16},{56,24},{64,96... | collective-permute-start | bytes 1572872 | tf_op jit(solution)/shard_map/ppermute | solution.py:10
  144.5 177.9 %copy-start.1 = (bf16[128,128]{1,0:T(8,128)(2,1)S(1)}, bf16[128,128]{1,0:T(8,128)(2,1)}, u32[]{:S(2)}) copy-start(bf16[128,128]{1,0:T(8,128)(2,1)} %param.8) | copy-start | bytes 98308
  206.5 555.7 %all-reduce.2.cloned.1.call-start = ((), (), s32[]{:S(2)}) async-start(), calls=%async_computation.2 | async-start | bytes 131072 | tf_op jit(solution)/shard_map/psum | solution.py:78
Sparse Core Ops, SparseCore 0:
  206.6 44.0 reduce-scatter.1
  322.5 439.6 all-reduce.1
where the time goes:
time: 772 us; the launch traced here: 771 us
  waiting for transfers between devices  526 us (68%)
  blocking collectives  134 us (17%)
  starting transfers between devices  37.3 us (5%)
  matrix products  27.8 us (4%)
  other arithmetic  25.4 us (3%)
  between operations  14.3 us (2%)
    psum x1, waiting for transfers between devices, body(): lax.psum((weight_local, bias_local), ('dom', 'rep'))  438 us
    psum x1, blocking collectives, body(): lax.psum((weight_local, bias_local), ('dom', 'rep'))  114 us
    ppermute x8, waiting for transfers between devices, swapped(): return lax.ppermute(value, axis, pairs)  87.7 us
    ppermute x8, starting transfers between devices, swapped(): return lax.ppermute(value, axis, pairs)  37.2 us
    scatter-add x5, other arithmetic, partial_panel(): placed.at[targets]  20.9 us
    all_gather x1, blocking collectives, body(): own_rows = lax.all_gather(projected, 'rep', axis=0, tiled=True)  19.5 us
  transfers between devices with their start and end apart: 10, of which 5 were waited for; matrix products, arithmetic and copies ran while one was open for 4% of the time, Pallas kernels for 0%

commit v1 on v0

v1 whole, which is shorter than its diff:
```python
import jax
import jax.numpy as jnp
from jax import lax
from jax.experimental import pallas as pl
from jax.experimental.pallas import tpu as pltpu
from jax.sharding import PartitionSpec as P

MESH = pl.DeviceIdType.MESH
F32 = jnp.float32
BF16 = jnp.bfloat16
ROWS = 16


def tree_sum(parts):
    while len(parts) > 1:
        parts = [parts[i] + parts[i + 1] for i in range(0, len(parts), 2)]
    return parts[0]


def kernel(
    dom_size, rep_size, y_size,
    feats, weight, bias, tiles, cols, count, cot,
    hidden_o, gw_o, gb_o, gf_o,
    tl, adj, xbuf, pbuf, rbuf, zsend, zrecv, w_v, b_v, cot_v, cols_s, count_s,
    gsend, grecv, asend, arecv, gfull,
    lsem, xs, xr, ps, pr, fzs, fzr, bzs, bzr, gs, gr, as_, ar, ns, nr,
):
    slots, max_tiles, block = tl.shape[0], tl.shape[1], tl.shape[2]
    dom, rep = lax.axis_index("dom"), lax.axis_index("rep")

    def zpeer(k):
        return (jnp.bitwise_xor(dom, dom_size >> k), rep)

    def rpeer(j):
        return (dom, jnp.bitwise_xor(rep, j))

    z_lo = [1 * y_size, 2 * y_size, 3 * y_size]
    z_hi = [4 * y_size, 8 * y_size, 12 * y_size]
    stages = [[1, 2, 3], z_lo, z_hi]
    far = sorted(set(sum(stages, [])) | {dom_size >> k for k in range(1, slots)})

    loc = [
        pltpu.make_async_copy(feats, xbuf.at[0, 0], lsem.at[0]),
        pltpu.make_async_copy(cols.at[0], cols_s, lsem.at[1]),
        pltpu.make_async_copy(count, count_s, lsem.at[2]),
    ]
    order = [0] + list(range(slots - 1, 0, -1))
    tcopy = {k: pltpu.make_async_copy(tiles.at[0, k], tl.at[k], lsem.at[6 + k]) for k in order}
    late = [
        pltpu.make_async_copy(weight, w_v, lsem.at[3]),
        pltpu.make_async_copy(bias, b_v, lsem.at[4]),
        pltpu.make_async_copy(cot, cot_v, lsem.at[5]),
    ]
    for c in loc:
        c.start()
    for k in order:
        tcopy[k].start()
    for c in late:
        c.start()

    barrier = pltpu.get_barrier_semaphore()
    for m in far:
        pl.semaphore_signal(barrier, inc=1, device_id=(jnp.bitwise_xor(dom, m), rep), device_id_type=MESH)
    for j in range(1, rep_size):
        pl.semaphore_signal(barrier, inc=1, device_id=rpeer(j), device_id_type=MESH)

    for c in loc[1:]:
        c.wait()
    chunks = block // ROWS
    width = max_tiles * ROWS
    lane = lax.broadcasted_iota(jnp.int32, (rep_size * ROWS, width), 1)
    row = lax.broadcasted_iota(jnp.int32, (rep_size * ROWS, width), 0)
    diag = (lane & (ROWS - 1)) == (row & (ROWS - 1))
    row_col = row >> (ROWS.bit_length() - 1)
    lane_1 = lax.broadcasted_iota(jnp.int32, (8, width), 1) >> (ROWS.bit_length() - 1)

    def build(k):
        live = count_s[0, k]
        want = jnp.full((8, width), -1, jnp.int32)
        for m in range(max_tiles):
            col = jnp.where(m < live, jnp.bitwise_xor(cols_s[k, m], rep), -1)
            want = jnp.where(lane_1 == m, col, want)
        want = jnp.broadcast_to(want[0:1], (rep_size * ROWS, width))
        sel = jnp.where(diag & (want == row_col), 1.0, 0.0).astype(BF16)
        tcopy[k].wait()
        for c in range(chunks):
            part = tl[k, :, c * ROWS:(c + 1) * ROWS, :].reshape(width, block)
            out = jnp.dot(sel, part, preferred_element_type=F32).astype(BF16)
            for j in range(rep_size):
                adj[k, c * ROWS:(c + 1) * ROWS, j * block:(j + 1) * block] = out[j * ROWS:(j + 1) * ROWS]

    def remote(src, dst, ssem, rsem, peer):
        return pltpu.make_async_remote_copy(
            src_ref=src, dst_ref=dst, send_sem=ssem, recv_sem=rsem, device_id=peer, device_id_type=MESH
        )

    build(order[0])
    build(order[1])
    build(order[2])
    loc[0].wait()
    pl.semaphore_wait(barrier, len(far) + rep_size - 1)

    fz = {}
    for k in range(1, slots):
        fz[k] = remote(xbuf.at[0, 0], xbuf.at[k, 0], fzs.at[k], fzr.at[k], zpeer(k))
        fz[k].start()
    fx = {}

    def spread(k):
        fx[k] = []
        for j in range(1, rep_size):
            c = remote(xbuf.at[k, 0], xbuf.at[k, j], xs.at[k, j], xr.at[k, j], rpeer(j))
            c.start()
            fx[k].append(c)

    def product(k):
        for c in fx[k]:
            c.wait_recv()
        x = xbuf[k].reshape(rep_size * block, block)
        return jnp.dot(adj[k], x, preferred_element_type=F32)

    spread(0)
    for k in order[3:]:
        build(k)
    total = product(0)
    for k in order[1:]:
        fz[k].wait_recv()
        spread(k)
        if k != order[1]:
            total = total + product(k + 1)
    for c in late:
        c.wait()
    total = total + product(order[-1])

    t_hi = total.astype(BF16)
    t_lo = (total - t_hi.astype(F32)).astype(BF16)
    w = w_v[...]
    v = jnp.dot(t_hi, w, preferred_element_type=F32) + jnp.dot(t_lo, w, preferred_element_type=F32) + b_v[...]
    c0 = 0.7978845608028654
    th = jnp.tanh(c0 * (v + 0.044715 * (v * v * v)))
    cdf = 0.5 * (1.0 + th)
    deriv = cdf + 0.5 * v * (1.0 - th * th) * (c0 * (1.0 + 3.0 * 0.044715 * v * v))
    grad_pre = cot_v[...].astype(F32) * deriv
    g = grad_pre.astype(BF16)
    back = lax.dot_general(w, g, (((1,), (1,)), ((), ())), preferred_element_type=F32).astype(BF16)

    bx = {}
    own = {}

    def push(k):
        part = jnp.dot(back, adj[k], preferred_element_type=F32)
        own[k] = part[:, :block]
        bx[k] = []
        for j in range(1, rep_size):
            pbuf[k, j] = part[:, j * block:(j + 1) * block].astype(BF16)
            c = remote(pbuf.at[k, j], rbuf.at[k, j], ps.at[k, j], pr.at[k, j], rpeer(j))
            c.start()
            bx[k].append(c)
        pbuf[k, 0] = own[k].astype(BF16)

    def gathered(k):
        parts = [pbuf[k, 0].astype(F32)]
        for j in range(1, rep_size):
            bx[k][j - 1].wait_recv()
            parts.append(rbuf[k, j].astype(F32))
        return tree_sum(parts)

    push(1)
    gw = lax.dot_general(t_hi, g, (((0,), (0,)), ((), ())), preferred_element_type=F32) + lax.dot_general(
        t_lo, g, (((0,), (0,)), ((), ())), preferred_element_type=F32
    )
    piece = block // rep_size
    gb = jnp.broadcast_to(jnp.sum(grad_pre, axis=0, keepdims=True), (8, block))
    for p in range(rep_size):
        gsend[p, 0:piece, :] = gw[p * piece:(p + 1) * piece]
        gsend[p, piece:, :] = gb
    gx = []
    for j in range(1, rep_size):
        c = remote(gsend.at[jnp.bitwise_xor(rep, j)], grecv.at[j], gs.at[j], gr.at[j], rpeer(j))
        c.start()
        gx.append(c)
    for k in range(2, slots):
        push(k)
    push(0)
    hidden_o[...] = (v * cdf).astype(BF16)

    bz = {}

    def cross(k):
        zsend[k] = gathered(k).astype(BF16)
        bz[k] = remote(zsend.at[k], zrecv.at[k], bzs.at[k], bzr.at[k], zpeer(k))
        bz[k].start()

    ax = []

    def stage(s, value):
        asend[s] = value
        ax.append([])
        for i, m in enumerate(stages[s]):
            c = remote(
                asend.at[s], arecv.at[s, i], as_.at[s, i], ar.at[s, i], (jnp.bitwise_xor(dom, m), rep)
            )
            c.start()
            ax[s].append(c)

    def staged(s):
        for c in ax[s]:
            c.wait_recv()
        return tree_sum([asend[s], arecv[s, 0], arecv[s, 1], arecv[s, 2]])

    cross(1)
    parts = [gsend[rep]]
    for j in range(1, rep_size):
        gx[j - 1].wait_recv()
        parts.append(grecv[j])
    stage(0, tree_sum(parts))
    cross(2)
    stage(1, staged(0))
    cross(3)
    stage(2, staged(1))
    cross(4)
    acc = gathered(0)
    whole = staged(2)
    gfull[rep] = whole[0:piece]
    nx = []
    for j in range(1, rep_size):
        c = remote(gfull.at[rep], gfull.at[rep], ns.at[j], nr.at[j], rpeer(j))
        c.start()
        nx.append(c)
    gb_o[...] = whole[piece:piece + 1]
    for k in range(slots - 1, 0, -1):
        bz[k].wait_recv()
        acc = acc + zrecv[k].astype(F32)
    gf_o[...] = acc.T.astype(BF16)
    for c in nx:
        c.wait_recv()
    gw_o[...] = gfull[...].reshape(block, block)

    for k in range(1, slots):
        fz[k].wait_send()
        bz[k].wait_send()
    for k in range(slots):
        for c in fx[k] + bx[k]:
            c.wait_send()
    for c in gx + nx + ax[0] + ax[1] + ax[2]:
        c.wait_send()


def solution(mesh):
    dom_size, rep_size = mesh.shape["dom"], mesh.shape["rep"]
    y_size = 4

    def body(feats, weight, bias, tiles, tile_cols, tile_count, cot):
        slots, max_tiles, block = tiles.shape[1], tiles.shape[2], tiles.shape[3]
        dma = pltpu.SemaphoreType.DMA
        vmem = pltpu.VMEM
        piece = block // rep_size
        any_spec = pl.BlockSpec(memory_space=pl.ANY)
        out_spec = pl.BlockSpec(memory_space=pltpu.VMEM)
        outs = pl.pallas_call(
            lambda *refs: kernel(dom_size, rep_size, y_size, *refs),
            out_shape=(
                jax.ShapeDtypeStruct((block, block), BF16),
                jax.ShapeDtypeStruct((block, block), F32),
                jax.ShapeDtypeStruct((1, block), F32),
                jax.ShapeDtypeStruct((block, block), BF16),
            ),
            in_specs=[any_spec] * 7,
            out_specs=(out_spec,) * 4,
            scratch_shapes=[
                vmem((slots, max_tiles, block, block), BF16),
                vmem((slots, block, rep_size * block), BF16),
                vmem((slots, rep_size, block, block), BF16),
                vmem((slots, rep_size, block, block), BF16),
                vmem((slots, rep_size, block, block), BF16),
                vmem((slots, block, block), BF16),
                vmem((slots, block, block), BF16),
                vmem((block, block), BF16),
                vmem((1, block), F32),
                vmem((block, block), BF16),
                pltpu.SMEM((slots, max_tiles), jnp.int32),
                pltpu.SMEM((1, slots), jnp.int32),
                vmem((rep_size, piece + 8, block), F32),
                vmem((rep_size, piece + 8, block), F32),
                vmem((3, piece + 8, block), F32),
                vmem((3, 3, piece + 8, block), F32),
                vmem((rep_size, piece, block), F32),
                dma((6 + slots,)),
                dma((slots, rep_size)), dma((slots, rep_size)),
                dma((slots, rep_size)), dma((slots, rep_size)),
                dma((slots,)), dma((slots,)), dma((slots,)), dma((slots,)),
                dma((rep_size,)), dma((rep_size,)),
                dma((3, 3)), dma((3, 3)),
                dma((rep_size,)), dma((rep_size,)),
            ],
            compiler_params=pltpu.CompilerParams(collective_id=0, has_side_effects=True),
            name="gcn_step",
        )(feats, weight, bias.reshape(1, block), tiles, tile_cols, tile_count, cot)
        return outs[0], outs[1], outs[2].reshape(block), outs[3]

    return jax.shard_map(
        body,
        mesh=mesh,
        in_specs=(
            P(("dom", "rep"), None),
            P(),
            P(),
            P(("dom", "rep"), None, None, None, None),
            P(("dom", "rep"), None, None),
            P(("dom", "rep"), None),
            P(("dom", "rep"), None),
        ),
        out_specs=(P(("dom", "rep"), None), P(), P(), P(("dom", "rep"), None)),
        check_vma=False,
    )
```

time: 772 us -> 74.2 us (0.10)
  waiting for transfers between devices: 526 us -> 0 us
  blocking collectives: 134 us -> 0 us
  Pallas kernels: 0 us -> 66.6 us
  starting transfers between devices: 37.3 us -> 0 us
  matrix products: 27.8 us -> 0 us
  other arithmetic: 25.4 us -> 0 us
  between operations: 14.3 us -> 0.64 us
    psum x1 -> x0, waiting for transfers between devices: 438 us -> none  [body(): lax.psum((weight_local, bias_local), ('dom', 'rep'))]
    psum x1 -> x0, blocking collectives: 114 us -> none  [body(): lax.psum((weight_local, bias_local), ('dom', 'rep'))]
    ppermute x8 -> x0, waiting for transfers between devices: 87.7 us -> none  [swapped(): return lax.ppermute(value, axis, pairs)]
    pallas_call x0 -> x1, Pallas kernels: none -> 66.6 us  [body(): pl.pallas_call(lambda *refs: kernel(dom_size, rep_size, y_size, *refs), o...]
    ppermute x8 -> x0, starting transfers between devices: 37.2 us -> none  [swapped(): return lax.ppermute(value, axis, pairs)]
    dot_general x13 -> x0, matrix products: 27.8 us -> none  [the longest x5 14.8 us: partial_panel(): jnp.einsum('tmij,tih->tmjh', masked, grad_rows_b, preferred_element_type=...]
    scatter-add x5 -> x0, other arithmetic: 20.9 us -> none  [partial_panel(): placed.at[targets]]
    all_gather x1 -> x0, blocking collectives: 19.5 us -> none  [body(): own_rows = lax.all_gather(projected, 'rep', axis=0, tiled=True)]
  transfers between devices with their start and end apart: 10 -> 0, of which waited for: 5 -> 0; matrix products, arithmetic and copies ran while one was open for 4% -> 0% of each run, Pallas kernels for 0% -> 0%
where the time goes in v1:
time: 74.2 us; the launch traced here: 73.9 us
  Pallas kernels  66.6 us (90%)
  local copies, waits for them, and re-layouts  6.67 us (9%)
    pallas_call x1, Pallas kernels, body(): pl.pallas_call(lambda *refs: kernel(dom_size, rep_size, y_size, *refs), o...  66.6 us
    unnamed x5, local copies, waits for them, and re-layouts  6.67 us

profile of v1, /device:TPU:1, one launch (start us, length us, event | category | flops | bytes accessed | tf_op | source)
XLA Modules:
  0.0 73.9 jit_solution(12789482547789228831)
XLA Ops:
  0.6 1.3 %copy.11.refs_4_ = s32[1,5,28]{2,1,0:T(8,128)} copy(s32[1,5,28]{2,0,1:T(1,128)} %param.11) | data formatting | bytes 1120 | tf_op args[4]
  1.9 66.6 %gcn_step.1 = (bf16[128,128]{1,0:T(8,128)(2,1)}, f32[128,128]{1,0:T(8,128)}, f32[1,128]{1,0:T(1,128)}, bf16[128,128]{1,0:T(8,128)(2,1)}) custom-call(bf16[128,128]{1,0:T(8,128)(2,1)} %refs_0_.1, bf16[128,128]{1,0:T(8,128)(2,1)} %refs_1_.1, f32[1,128]{1,0:T(1,128)} %bitcast.2, bf16[1,5,28,128,128]{4,3,2,1,0:T(8,128)(2,1)} %refs_3_.1, ...), custom_call_target="tpu_custom_call" | custom-call | tf_op jit(solution)/shard_map/gcn_step/pallas_call | solution.py:260
  68.5 1.4 %copy.16 = bf16[128,128]{1,0:T(8,128)(2,1)} copy(bf16[128,128]{1,0:T(8,128)(2,1)} %get-tuple-element.16) | data formatting | bytes 65536
  69.8 1.5 %copy.17 = f32[128,128]{1,0:T(8,128)} copy(f32[128,128]{1,0:T(8,128)} %get-tuple-element.17) | data formatting | bytes 131072
  71.3 1.2 %copy.18 = f32[128]{0:T(128)} copy(f32[128]{0:T(128)} %bitcast.3) | data formatting | bytes 1024
  72.5 1.4 %copy.19 = bf16[128,128]{1,0:T(8,128)(2,1)} copy(bf16[128,128]{1,0:T(8,128)(2,1)} %get-tuple-element.19) | data formatting | bytes 65536

commit v2 on v1

v2 whole, which is shorter than its diff:
```python
import jax
import jax.numpy as jnp
from jax import lax
from jax.experimental import pallas as pl
from jax.experimental.pallas import tpu as pltpu
from jax.sharding import PartitionSpec as P

MESH = pl.DeviceIdType.MESH
F32 = jnp.float32
BF16 = jnp.bfloat16
ROWS = 16


def tree_sum(parts):
    while len(parts) > 1:
        parts = [parts[i] + parts[i + 1] for i in range(0, len(parts), 2)]
    return parts[0]


def kernel(
    dom_size, rep_size, y_size,
    feats, weight, bias, tiles, cols, count, cot,
    hidden_o, gw_o, gb_o, gf_o,
    tl, adj, xbuf, pown, psib, qbuf, rsend, rbuf, zsend, zrecv, w_v, b_v, cot_v, cols_s, count_s,
    gsend, grecv, asend, arecv,
    lsem, xs, xr, sibs, sibr, qs, qr, ps, pr, fzs, fzr, bzs, bzr, gs, gr, as_, ar, ns, nr,
):
    slots, max_tiles, block = tl.shape[0], tl.shape[1], tl.shape[2]
    chips = rep_size // 2
    dom, rep = lax.axis_index("dom"), lax.axis_index("rep")
    sibling = (dom, jnp.bitwise_xor(rep, 1))

    def zpeer(k):
        return (jnp.bitwise_xor(dom, dom_size >> k), rep)

    def rpeer(j):
        return (dom, jnp.bitwise_xor(rep, j))

    z_lo = [1 * y_size, 2 * y_size, 3 * y_size]
    z_hi = [4 * y_size, 8 * y_size, 12 * y_size]
    stages = [[1, 2, 3], z_lo, z_hi]
    far = sorted(set(sum(stages, [])) | {dom_size >> k for k in range(1, slots)})

    barrier = pltpu.get_barrier_semaphore()
    for m in far[::-1]:
        pl.semaphore_signal(barrier, inc=1, device_id=(jnp.bitwise_xor(dom, m), rep), device_id_type=MESH)
    for j in range(1, rep_size):
        pl.semaphore_signal(barrier, inc=1, device_id=rpeer(j), device_id_type=MESH)

    loc = [
        pltpu.make_async_copy(feats, xbuf.at[0, 0, 0], lsem.at[0]),
        pltpu.make_async_copy(cols, cols_s, lsem.at[1]),
        pltpu.make_async_copy(count, count_s, lsem.at[2]),
    ]
    order = [0] + list(range(slots - 1, 0, -1))
    tcopy = {k: pltpu.make_async_copy(tiles.at[0, k], tl.at[k], lsem.at[6 + k]) for k in order}
    late = [
        pltpu.make_async_copy(weight, w_v, lsem.at[3]),
        pltpu.make_async_copy(bias, b_v, lsem.at[4]),
        pltpu.make_async_copy(cot, cot_v, lsem.at[5]),
    ]
    for c in loc:
        c.start()
    for k in order:
        tcopy[k].start()
    for c in late:
        c.start()

    def remote(_, src, dst, ssem, rsem, peer):
        return pltpu.make_async_remote_copy(
            src_ref=src, dst_ref=dst, send_sem=ssem, recv_sem=rsem, device_id=peer, device_id_type=MESH
        )

    sent = []

    def go(*args):
        c = remote(*args)
        c.start()
        sent.append(c)
        return c

    chunks = block // ROWS
    width = max_tiles * ROWS
    lane = lax.broadcasted_iota(jnp.int32, (rep_size * ROWS, width), 1)
    row = lax.broadcasted_iota(jnp.int32, (rep_size * ROWS, width), 0)
    diag = (lane & (ROWS - 1)) == (row & (ROWS - 1))
    row_col = row >> (ROWS.bit_length() - 1)
    lane_1 = lax.broadcasted_iota(jnp.int32, (8, width), 1) >> (ROWS.bit_length() - 1)

    def build(k):
        live = count_s[0, k]
        want = jnp.full((8, width), -1, jnp.int32)
        for m in range(max_tiles):
            e = jnp.bitwise_xor(cols_s[k, 0, m], rep)
            col = jnp.where(m < live, (e & 1) * chips + (e >> 1), -1)
            want = jnp.where(lane_1 == m, col, want)
        want = jnp.broadcast_to(want[0:1], (rep_size * ROWS, width))
        sel = jnp.where(diag & (want == row_col), 1.0, 0.0).astype(BF16)
        tcopy[k].wait()
        for c in range(chunks):
            part = tl[k, :, c * ROWS:(c + 1) * ROWS, :].reshape(width, block)
            out = jnp.dot(sel, part, preferred_element_type=F32).astype(BF16)
            for j in range(rep_size):
                adj[k, c * ROWS:(c + 1) * ROWS, j * block:(j + 1) * block] = out[j * ROWS:(j + 1) * ROWS]

    half = chips * block
    fz, fx, fs = {}, {}, {}

    def spread(k):
        fx[k] = [
            go("X", xbuf.at[k, 0, 0], xbuf.at[k, 0, i], xs.at[k, i], xr.at[k, i], rpeer(2 * i)) for i in range(1, chips)
        ]

    def share(k):
        for c in fx[k]:
            c.wait_recv()
        fs[k] = go("X", xbuf.at[k, 0], xbuf.at[k, 1], sibs.at[k], sibr.at[k], sibling)

    def product(k, h):
        if h == 1:
            fs[k].wait_recv()
        return jnp.dot(
            adj[k, :, h * half:(h + 1) * half], xbuf[k, h].reshape(half, block), preferred_element_type=F32
        )

    loc[0].wait()
    pl.semaphore_wait(barrier, len(far) + rep_size - 1)
    for k in range(1, slots):
        fz[k] = go("F", xbuf.at[0, 0, 0], xbuf.at[k, 0, 0], fzs.at[k], fzr.at[k], zpeer(k))
    spread(0)
    for c in loc[1:]:
        c.wait()
    build(0)
    fz[4].wait_recv()
    spread(4)
    fz[3].wait_recv()
    spread(3)
    build(4)
    share(0)
    build(3)
    fz[2].wait_recv()
    spread(2)
    share(4)
    build(2)
    share(3)
    build(1)
    total = product(0, 0) + product(0, 1) + product(4, 0) + product(4, 1)
    share(2)
    fz[1].wait_recv()
    spread(1)
    total = total + product(3, 0) + product(3, 1) + product(2, 0) + product(2, 1)
    for c in late:
        c.wait()
    share(1)
    total = total + product(1, 0)
    total = total + product(1, 1)

    t_hi = total.astype(BF16)
    t_lo = (total - t_hi.astype(F32)).astype(BF16)
    w = w_v[...]
    v = jnp.dot(t_hi, w, preferred_element_type=F32) + jnp.dot(t_lo, w, preferred_element_type=F32) + b_v[...]
    c0 = 0.7978845608028654
    th = jnp.tanh(c0 * (v + 0.044715 * (v * v * v)))
    cdf = 0.5 * (1.0 + th)
    deriv = cdf + 0.5 * v * (1.0 - th * th) * (c0 * (1.0 + 3.0 * 0.044715 * v * v))
    grad_pre = cot_v[...].astype(F32) * deriv
    g = grad_pre.astype(BF16)

    gw = lax.dot_general(t_hi, g, (((0,), (0,)), ((), ())), preferred_element_type=F32) + lax.dot_general(
        t_lo, g, (((0,), (0,)), ((), ())), preferred_element_type=F32
    )
    piece = block // rep_size
    gb = jnp.broadcast_to(jnp.sum(grad_pre, axis=0, keepdims=True), (8, block))
    for p in range(rep_size):
        gsend[p, 0:piece, :] = gw[p * piece:(p + 1) * piece]
        gsend[p, piece:, :] = gb
    gx = [
        go("G", gsend.at[jnp.bitwise_xor(rep, j)], grecv.at[j], gs.at[j], gr.at[j], rpeer(j)) for j in range(1, rep_size)
    ]

    back = lax.dot_general(w, g, (((1,), (1,)), ((), ())), preferred_element_type=F32).astype(BF16)
    bq, bx, bz = {}, {}, {}

    def push(k):
        part = jnp.dot(back, adj[k, :, half:], preferred_element_type=F32)
        for i in range(chips):
            psib[k, i] = part[:, i * block:(i + 1) * block].astype(BF16)
        bq[k] = go("B", psib.at[k], qbuf.at[k], qs.at[k], qr.at[k], sibling)
        part = jnp.dot(back, adj[k, :, :half], preferred_element_type=F32)
        for i in range(chips):
            pown[k, i] = part[:, i * block:(i + 1) * block]

    def pair(k):
        bq[k].wait_recv()
        bx[k] = []
        for i in range(1, chips):
            rsend[k, i] = (pown[k, i] + qbuf[k, i].astype(F32)).astype(BF16)
            bx[k].append(go("B", rsend.at[k, i], rbuf.at[k, i], ps.at[k, i], pr.at[k, i], rpeer(2 * i)))

    def gathered(k):
        part = pown[k, 0] + qbuf[k, 0].astype(F32)
        for i in range(1, chips):
            bx[k][i - 1].wait_recv()
            part = part + rbuf[k, i].astype(F32)
        return part

    def cross(k):
        zsend[k] = gathered(k).astype(BF16)
        bz[k] = go("Z", zsend.at[k], zrecv.at[k], bzs.at[k], bzr.at[k], zpeer(k))

    ax = []

    def stage(s, value):
        asend[s] = value
        ax.append([
            go("G", asend.at[s], arecv.at[s, i], as_.at[s, i], ar.at[s, i], (jnp.bitwise_xor(dom, m), rep))
            for i, m in enumerate(stages[s])
        ])

    def staged(s):
        for c in ax[s]:
            c.wait_recv()
        return tree_sum([asend[s], arecv[s, 0], arecv[s, 1], arecv[s, 2]])

    push(1)
    push(2)
    pair(1)
    push(3)
    parts = [gsend[rep]]
    for j in range(1, rep_size):
        gx[j - 1].wait_recv()
        parts.append(grecv[j])
    stage(0, tree_sum(parts))
    pair(2)
    push(4)
    pair(3)
    push(0)
    cross(1)
    stage(1, staged(0))
    pair(4)
    cross(2)
    pair(0)
    cross(3)
    cross(4)
    stage(2, staged(1))
    acc = gathered(0)
    hidden_o[...] = (v * cdf).astype(BF16)
    for k in range(slots - 1, 1, -1):
        bz[k].wait_recv()
        acc = acc + zrecv[k].astype(F32)
    bz[1].wait_recv()
    gf_o[...] = (acc + zrecv[1].astype(F32)).T.astype(BF16)
    whole = staged(2)
    gw_o[rep] = whole[0:piece]
    nx = [go("G", gw_o.at[rep], gw_o.at[rep], ns.at[j], nr.at[j], rpeer(j)) for j in range(1, rep_size)]
    gb_o[...] = whole[piece:piece + 1]
    for c in nx:
        c.wait_recv()
    for c in sent:
        c.wait_send()


def finish(hidden, gw, gb, gf, hidden_o, gw_o, gb_o, gf_o):
    hidden_o[...] = hidden[...]
    gw_o[...] = gw[...]
    gb_o[...] = gb[...]
    gf_o[...] = gf[...]


def solution(mesh):
    dom_size, rep_size = mesh.shape["dom"], mesh.shape["rep"]
    y_size = 4

    def body(feats, weight, bias, tiles, tile_cols, tile_count, cot):
        slots, max_tiles, block = tiles.shape[1], tiles.shape[2], tiles.shape[3]
        dma = pltpu.SemaphoreType.DMA
        vmem = pltpu.VMEM
        piece = block // rep_size
        chips = rep_size // 2
        any_spec = pl.BlockSpec(memory_space=pl.ANY)
        vmem_spec = pl.BlockSpec(memory_space=pltpu.VMEM)
        outs = pl.pallas_call(
            lambda *refs: kernel(dom_size, rep_size, y_size, *refs),
            out_shape=(
                vmem((block, block), BF16),
                vmem((rep_size, piece, block), F32),
                vmem((1, block), F32),
                vmem((block, block), BF16),
            ),
            in_specs=[any_spec] * 7,
            out_specs=(vmem_spec,) * 4,
            scratch_shapes=[
                vmem((slots, max_tiles, block, block), BF16),
                vmem((slots, block, rep_size * block), BF16),
                vmem((slots, 2, chips, block, block), BF16),
                vmem((slots, chips, block, block), F32),
                vmem((slots, chips, block, block), BF16),
                vmem((slots, chips, block, block), BF16),
                vmem((slots, chips, block, block), BF16),
                vmem((slots, chips, block, block), BF16),
                vmem((slots, block, block), BF16),
                vmem((slots, block, block), BF16),
                vmem((block, block), BF16),
                vmem((1, block), F32),
                vmem((block, block), BF16),
                pltpu.SMEM((slots, 1, max_tiles), jnp.int32),
                pltpu.SMEM((1, slots), jnp.int32),
                vmem((rep_size, piece + 8, block), F32),
                vmem((rep_size, piece + 8, block), F32),
                vmem((3, piece + 8, block), F32),
                vmem((3, 3, piece + 8, block), F32),
                dma((6 + slots,)),
                dma((slots, chips)), dma((slots, chips)),
                dma((slots,)), dma((slots,)), dma((slots,)), dma((slots,)),
                dma((slots, chips)), dma((slots, chips)),
                dma((slots,)), dma((slots,)), dma((slots,)), dma((slots,)),
                dma((rep_size,)), dma((rep_size,)),
                dma((3, 3)), dma((3, 3)),
                dma((rep_size,)), dma((rep_size,)),
            ],
            compiler_params=pltpu.CompilerParams(
                collective_id=0, has_side_effects=True
            ),
            name="gcn_step",
        )(feats, weight, bias.reshape(1, block), tiles, jnp.transpose(tile_cols, (1, 0, 2)), tile_count, cot)
        outs = pl.pallas_call(
            finish,
            out_shape=(
                jax.ShapeDtypeStruct((block, block), BF16),
                jax.ShapeDtypeStruct((block, block), F32),
                jax.ShapeDtypeStruct((1, block), F32),
                jax.ShapeDtypeStruct((block, block), BF16),
            ),
            in_specs=[vmem_spec] * 4,
            out_specs=(vmem_spec,) * 4,
            compiler_params=pltpu.CompilerParams(vmem_limit_bytes=2**20),
            name="finish",
        )(outs[0], outs[1].reshape(block, block), outs[2], outs[3])
        return outs[0], outs[1], outs[2].reshape(block), outs[3]

    return jax.shard_map(
        body,
        mesh=mesh,
        in_specs=(
            P(("dom", "rep"), None),
            P(),
            P(),
            P(("dom", "rep"), None, None, None, None),
            P(("dom", "rep"), None, None),
            P(("dom", "rep"), None),
            P(("dom", "rep"), None),
        ),
        out_specs=(P(("dom", "rep"), None), P(), P(), P(("dom", "rep"), None)),
        check_vma=False,
    )
```

time: 74.2 us -> 60.7 us (0.82)
  Pallas kernels: 66.6 us -> 59.9 us
  local copies, waits for them, and re-layouts: 6.67 us -> 0 us
    pallas_call x1, Pallas kernels: 66.6 us -> 59.3 us  [body(): pl.pallas_call(lambda *refs: kernel(dom_size, rep_size, y_size, *refs), o...]
    unnamed x5 -> x0, local copies, waits for them, and re-layouts: 6.67 us -> none
where the time goes in v2:
time: 60.7 us; the launch traced here: 60.6 us
  Pallas kernels  59.9 us (99%)
  between operations  0.64 us (1%)
    pallas_call x1, Pallas kernels, body(): pl.pallas_call(lambda *refs: kernel(dom_size, rep_size, y_size, *refs), o...  59.3 us

profile of v2, /device:TPU:1, one launch (start us, length us, event | category | flops | bytes accessed | tf_op | source)
XLA Modules:
  0.0 60.6 jit_solution(27922830788396172)
XLA Ops:
  0.6 59.3 %gcn_step.1 = (bf16[128,128]{1,0:T(8,128)(2,1)S(1)}, f32[8,16,128]{2,1,0:T(8,128)S(1)}, f32[1,128]{1,0:T(1,128)S(1)}, bf16[128,128]{1,0:T(8,128)(2,1)S(1)}) custom-call(bf16[128,128]{1,0:T(8,128)(2,1)} %refs_0_.1, bf16[128,128]{1,0:T(8,128)(2,1)} %refs_1_.1, f32[1,128]{1,0:T(1,128)} %bitcast.6, bf16[1,5,28,128,128]{4,3,2,1,0:T(8,128)(2,1)} %refs_3_.1, ...), custom_call_target="tpu_custom_call" | custom-call | tf_op jit(solution)/shard_map/gcn_step/pallas_call | solution.py:282
  59.9 0.7 %finish.1 = (bf16[128,128]{1,0:T(8,128)(2,1)}, f32[128,128]{1,0:T(8,128)}, f32[1,128]{1,0:T(1,128)}, bf16[128,128]{1,0:T(8,128)(2,1)}) custom-call(bf16[128,128]{1,0:T(8,128)(2,1)S(1)} %get-tuple-element.12.hidden, f32[128,128]{1,0:T(8,128)S(1)} %bitcast.4, f32[1,128]{1,0:T(1,128)S(1)} %get-tuple-element.14.gb, bf16[128,128]{1,0:T(8,128)(2,1)S(1)} %get-tuple-element.15.gf), custom_call_target="tpu_custom_call" | custom-call | tf_op jit(solution)/shard_map/finish/pallas_call | solution.py:326

commit v3 on v2

--- a/solution.py
+++ b/solution.py
@@ -22,8 +22,8 @@
     feats, weight, bias, tiles, cols, count, cot,
     hidden_o, gw_o, gb_o, gf_o,
     tl, adj, xbuf, pown, psib, qbuf, rsend, rbuf, zsend, zrecv, w_v, b_v, cot_v, cols_s, count_s,
-    gsend, grecv, asend, arecv,
-    lsem, xs, xr, sibs, sibr, qs, qr, ps, pr, fzs, fzr, bzs, bzr, gs, gr, as_, ar, ns, nr,
+    gsend, grecv, asend, arecv, whole_v, full_v,
+    lsem, xr, sibr, qr, pr, fzr, bzr, gr, ssem,
 ):
     slots, max_tiles, block = tl.shape[0], tl.shape[1], tl.shape[2]
     chips = rep_size // 2
@@ -36,16 +36,22 @@
     def rpeer(j):
         return (dom, jnp.bitwise_xor(rep, j))
 
-    z_lo = [1 * y_size, 2 * y_size, 3 * y_size]
-    z_hi = [4 * y_size, 8 * y_size, 12 * y_size]
-    stages = [[1, 2, 3], z_lo, z_hi]
-    far = sorted(set(sum(stages, [])) | {dom_size >> k for k in range(1, slots)})
-
+    plane_size = y_size * rep_size
+    depth = dom_size // y_size
+    plane = jnp.bitwise_and(dom, y_size - 1) * rep_size + rep
+
+    def ppeer(q):
+        return (jnp.bitwise_xor(dom, q // rep_size), jnp.bitwise_xor(rep, q % rep_size))
+
+    def dpeer(m):
+        return (jnp.bitwise_xor(dom, m * y_size), rep)
+
+    near = [m for m in (depth // 4, 3 * depth // 4, 1, 2, 3)]
     barrier = pltpu.get_barrier_semaphore()
-    for m in far[::-1]:
-        pl.semaphore_signal(barrier, inc=1, device_id=(jnp.bitwise_xor(dom, m), rep), device_id_type=MESH)
-    for j in range(1, rep_size):
-        pl.semaphore_signal(barrier, inc=1, device_id=rpeer(j), device_id_type=MESH)
+    for m in near:
+        pl.semaphore_signal(barrier, inc=1, device_id=dpeer(m), device_id_type=MESH)
+    for q in range(plane_size - 1, 0, -1):
+        pl.semaphore_signal(barrier, inc=1, device_id=ppeer(q), device_id_type=MESH)
 
     loc = [
         pltpu.make_async_copy(feats, xbuf.at[0, 0, 0], lsem.at[0]),
@@ -71,13 +77,13 @@
             src_ref=src, dst_ref=dst, send_sem=ssem, recv_sem=rsem, device_id=peer, device_id_type=MESH
         )
 
-    sent = []
-
     def go(*args):
         c = remote(*args)
         c.start()
-        sent.append(c)
         return c
+
+    def arrived(_, ref, sem):
+        pltpu.make_async_copy(ref, ref, sem).wait()
 
     chunks = block // ROWS
     width = max_tiles * ROWS
@@ -104,53 +110,55 @@
                 adj[k, c * ROWS:(c + 1) * ROWS, j * block:(j + 1) * block] = out[j * ROWS:(j + 1) * ROWS]
 
     half = chips * block
-    fz, fx, fs = {}, {}, {}
 
     def spread(k):
-        fx[k] = [
-            go("X", xbuf.at[k, 0, 0], xbuf.at[k, 0, i], xs.at[k, i], xr.at[k, i], rpeer(2 * i)) for i in range(1, chips)
-        ]
+        for i in range(1, chips):
+            go("X", xbuf.at[k, 0, 0], xbuf.at[k, 0, i], ssem.at[1], xr.at[k], rpeer(2 * i))
 
     def share(k):
-        for c in fx[k]:
-            c.wait_recv()
-        fs[k] = go("X", xbuf.at[k, 0], xbuf.at[k, 1], sibs.at[k], sibr.at[k], sibling)
+        arrived("X", xbuf.at[k, 0, 1:], xr.at[k])
+        go("X", xbuf.at[k, 0], xbuf.at[k, 1], ssem.at[2], sibr.at[k], sibling)
+
+    def fetched(k):
+        arrived("F", xbuf.at[k, 0, 0], fzr.at[k])
 
     def product(k, h):
         if h == 1:
-            fs[k].wait_recv()
+            arrived("X", xbuf.at[k, 1], sibr.at[k])
         return jnp.dot(
             adj[k, :, h * half:(h + 1) * half], xbuf[k, h].reshape(half, block), preferred_element_type=F32
         )
 
     loc[0].wait()
-    pl.semaphore_wait(barrier, len(far) + rep_size - 1)
-    for k in range(1, slots):
-        fz[k] = go("F", xbuf.at[0, 0, 0], xbuf.at[k, 0, 0], fzs.at[k], fzr.at[k], zpeer(k))
+    pl.semaphore_wait(barrier, len(near) + plane_size - 1)
+    for k in range(2, slots):
+        go("F", xbuf.at[0, 0, 0], xbuf.at[k, 0, 0], ssem.at[0], fzr.at[k], zpeer(k))
     spread(0)
     for c in loc[1:]:
         c.wait()
     build(0)
-    fz[4].wait_recv()
+    fetched(4)
     spread(4)
-    fz[3].wait_recv()
+    fetched(3)
     spread(3)
+    share(0)
     build(4)
-    share(0)
+    fetched(2)
+    go("F", xbuf.at[2, 0, 0], xbuf.at[1, 0, 0], ssem.at[0], fzr.at[1], dpeer(3 * depth // 4))
+    spread(2)
     build(3)
-    fz[2].wait_recv()
-    spread(2)
     share(4)
+    share(3)
     build(2)
-    share(3)
     build(1)
     total = product(0, 0) + product(0, 1) + product(4, 0) + product(4, 1)
     share(2)
-    fz[1].wait_recv()
-    spread(1)
-    total = total + product(3, 0) + product(3, 1) + product(2, 0) + product(2, 1)
+    total = total + product(3, 0) + product(3, 1)
     for c in late:
         c.wait()
+    fetched(1)
+    spread(1)
+    total = total + product(2, 0) + product(2, 1)
     share(1)
     total = total + product(1, 0)
     total = total + product(1, 1)
@@ -169,95 +177,86 @@
     gw = lax.dot_general(t_hi, g, (((0,), (0,)), ((), ())), preferred_element_type=F32) + lax.dot_general(
         t_lo, g, (((0,), (0,)), ((), ())), preferred_element_type=F32
     )
-    piece = block // rep_size
     gb = jnp.broadcast_to(jnp.sum(grad_pre, axis=0, keepdims=True), (8, block))
-    for p in range(rep_size):
-        gsend[p, 0:piece, :] = gw[p * piece:(p + 1) * piece]
-        gsend[p, piece:, :] = gb
-    gx = [
-        go("G", gsend.at[jnp.bitwise_xor(rep, j)], grecv.at[j], gs.at[j], gr.at[j], rpeer(j)) for j in range(1, rep_size)
-    ]
+    low = lax.broadcasted_iota(jnp.int32, (8, block), 0) < 4
+    for p in range(0, plane_size, 2):
+        rows = gw[4 * p:4 * p + 8]
+        gsend[p] = jnp.where(low, rows, gb).astype(BF16)
+        gsend[p + 1] = jnp.where(low, gb, rows).astype(BF16)
+    for q in range(1, plane_size):
+        go("G", gsend.at[jnp.bitwise_xor(plane, q)], grecv.at[q], ssem.at[6], gr.at[0], ppeer(q))
 
     back = lax.dot_general(w, g, (((1,), (1,)), ((), ())), preferred_element_type=F32).astype(BF16)
-    bq, bx, bz = {}, {}, {}
 
     def push(k):
         part = jnp.dot(back, adj[k, :, half:], preferred_element_type=F32)
         for i in range(chips):
             psib[k, i] = part[:, i * block:(i + 1) * block].astype(BF16)
-        bq[k] = go("B", psib.at[k], qbuf.at[k], qs.at[k], qr.at[k], sibling)
+        go("B", psib.at[k], qbuf.at[k], ssem.at[3], qr.at[k], sibling)
         part = jnp.dot(back, adj[k, :, :half], preferred_element_type=F32)
         for i in range(chips):
             pown[k, i] = part[:, i * block:(i + 1) * block]
 
     def pair(k):
-        bq[k].wait_recv()
-        bx[k] = []
+        arrived("B", qbuf.at[k], qr.at[k])
         for i in range(1, chips):
             rsend[k, i] = (pown[k, i] + qbuf[k, i].astype(F32)).astype(BF16)
-            bx[k].append(go("B", rsend.at[k, i], rbuf.at[k, i], ps.at[k, i], pr.at[k, i], rpeer(2 * i)))
+            go("B", rsend.at[k, i], rbuf.at[k, i], ssem.at[4], pr.at[k], rpeer(2 * i))
 
     def gathered(k):
+        arrived("B", rbuf.at[k, 1:], pr.at[k])
         part = pown[k, 0] + qbuf[k, 0].astype(F32)
         for i in range(1, chips):
-            bx[k][i - 1].wait_recv()
             part = part + rbuf[k, i].astype(F32)
         return part
 
     def cross(k):
         zsend[k] = gathered(k).astype(BF16)
-        bz[k] = go("Z", zsend.at[k], zrecv.at[k], bzs.at[k], bzr.at[k], zpeer(k))
-
-    ax = []
-
-    def stage(s, value):
-        asend[s] = value
-        ax.append([
-            go("G", asend.at[s], arecv.at[s, i], as_.at[s, i], ar.at[s, i], (jnp.bitwise_xor(dom, m), rep))
-            for i, m in enumerate(stages[s])
-        ])
-
-    def staged(s):
-        for c in ax[s]:
-            c.wait_recv()
-        return tree_sum([asend[s], arecv[s, 0], arecv[s, 1], arecv[s, 2]])
+        go("Z", zsend.at[k], zrecv.at[k], ssem.at[5], bzr.at[k], zpeer(k))
 
     push(1)
     push(2)
     pair(1)
     push(3)
-    parts = [gsend[rep]]
-    for j in range(1, rep_size):
-        gx[j - 1].wait_recv()
-        parts.append(grecv[j])
-    stage(0, tree_sum(parts))
+    arrived("G", grecv.at[1:], gr.at[0])
+    asend[...] = tree_sum([gsend[plane].astype(F32)] + [grecv[q].astype(F32) for q in range(1, plane_size)]).astype(BF16)
+    for m in range(1, depth):
+        go("G", asend, arecv.at[m], ssem.at[7], gr.at[1], dpeer(m))
     pair(2)
     push(4)
     pair(3)
     push(0)
     cross(1)
-    stage(1, staged(0))
     pair(4)
+    pair(0)
     cross(2)
-    pair(0)
     cross(3)
     cross(4)
-    stage(2, staged(1))
     acc = gathered(0)
     hidden_o[...] = (v * cdf).astype(BF16)
-    for k in range(slots - 1, 1, -1):
-        bz[k].wait_recv()
+    arrived("G", arecv.at[1:], gr.at[1])
+    whole = tree_sum([asend[...].astype(F32)] + [arecv[m].astype(F32) for m in range(1, depth)])
+    whole_v[...] = whole
+    full_v[plane] = whole
+    for q in range(1, plane_size):
+        go("G", whole_v, full_v.at[plane], ssem.at[8], gr.at[2], ppeer(q))
+    gb_o[...] = jnp.where((plane & 1) == 0, whole[4:5], whole[0:1])
+    for k in range(slots - 1, 0, -1):
+        arrived("Z", zrecv.at[k], bzr.at[k])
         acc = acc + zrecv[k].astype(F32)
-    bz[1].wait_recv()
-    gf_o[...] = (acc + zrecv[1].astype(F32)).T.astype(BF16)
-    whole = staged(2)
-    gw_o[rep] = whole[0:piece]
-    nx = [go("G", gw_o.at[rep], gw_o.at[rep], ns.at[j], nr.at[j], rpeer(j)) for j in range(1, rep_size)]
-    gb_o[...] = whole[piece:piece + 1]
-    for c in nx:
-        c.wait_recv()
-    for c in sent:
-        c.wait_send()
+    gf_o[...] = acc.T.astype(BF16)
+    arrived("G", full_v.at[1:], gr.at[2])
+    for p in range(0, plane_size, 2):
+        gw_o[4 * p:4 * p + 8] = jnp.where(low, full_v[p], full_v[p + 1])
+    arrived("F", zsend.at[1:], ssem.at[0])
+    arrived("X", rsend.at[:, 1:], ssem.at[1])
+    arrived("X", psib, ssem.at[2])
+    arrived("B", psib, ssem.at[3])
+    arrived("B", rsend.at[:, 1:], ssem.at[4])
+    arrived("Z", zsend.at[1:], ssem.at[5])
+    arrived("G", grecv.at[1:], ssem.at[6])
+    arrived("G", arecv.at[1:], ssem.at[7])
+    arrived("G", full_v.at[1:], ssem.at[8])
 
 
 def finish(hidden, gw, gb, gf, hidden_o, gw_o, gb_o, gf_o):
@@ -275,7 +274,6 @@
         slots, max_tiles, block = tiles.shape[1], tiles.shape[2], tiles.shape[3]
         dma = pltpu.SemaphoreType.DMA
         vmem = pltpu.VMEM
-        piece = block // rep_size
         chips = rep_size // 2
         any_spec = pl.BlockSpec(memory_space=pl.ANY)
         vmem_spec = pl.BlockSpec(memory_space=pltpu.VMEM)
@@ -283,7 +281,7 @@
             lambda *refs: kernel(dom_size, rep_size, y_size, *refs),
             out_shape=(
                 vmem((block, block), BF16),
-                vmem((rep_size, piece, block), F32),
+                vmem((block, block), F32),
                 vmem((1, block), F32),
                 vmem((block, block), BF16),
             ),
@@ -305,18 +303,15 @@
                 vmem((block, block), BF16),
                 pltpu.SMEM((slots, 1, max_tiles), jnp.int32),
                 pltpu.SMEM((1, slots), jnp.int32),
-                vmem((rep_size, piece + 8, block), F32),
-                vmem((rep_size, piece + 8, block), F32),
-                vmem((3, piece + 8, block), F32),
-                vmem((3, 3, piece + 8, block), F32),
+                vmem((y_size * rep_size, 8, block), BF16),
+                vmem((y_size * rep_size, 8, block), BF16),
+                vmem((8, block), BF16),
+                vmem((dom_size // y_size, 8, block), BF16),
+                vmem((8, block), F32),
+                vmem((y_size * rep_size, 8, block), F32),
                 dma((6 + slots,)),
-                dma((slots, chips)), dma((slots, chips)),
-                dma((slots,)), dma((slots,)), dma((slots,)), dma((slots,)),
-                dma((slots, chips)), dma((slots, chips)),
-                dma((slots,)), dma((slots,)), dma((slots,)), dma((slots,)),
-                dma((rep_size,)), dma((rep_size,)),
-                dma((3, 3)), dma((3, 3)),
-                dma((rep_size,)), dma((rep_size,)),
+                dma((slots,)), dma((slots,)), dma((slots,)), dma((slots,)), dma((slots,)), dma((slots,)),
+                dma((3,)), dma((9,)),
             ],
             compiler_params=pltpu.CompilerParams(
                 collective_id=0, has_side_effects=True
@@ -335,7 +330,7 @@
             out_specs=(vmem_spec,) * 4,
             compiler_params=pltpu.CompilerParams(vmem_limit_bytes=2**20),
             name="finish",
-        )(outs[0], outs[1].reshape(block, block), outs[2], outs[3])
+        )(outs[0], outs[1], outs[2], outs[3])
         return outs[0], outs[1], outs[2].reshape(block), outs[3]
 
     return jax.shard_map(

time: 60.7 us -> 53.8 us (0.89)
  Pallas kernels: 59.9 us -> 53 us
    pallas_call x1, Pallas kernels: 59.3 us -> 52.4 us  [body(): pl.pallas_call(lambda *refs: kernel(dom_size, rep_size, y_size, *refs), o...]
where the time goes in v3:
time: 53.8 us; the launch traced here: 53.7 us
  Pallas kernels  53 us (99%)
  between operations  0.64 us (1%)
    pallas_call x1, Pallas kernels, body(): pl.pallas_call(lambda *refs: kernel(dom_size, rep_size, y_size, *refs), o...  52.4 us

profile of v3, /device:TPU:1, one launch (start us, length us, event | category | flops | bytes accessed | tf_op | source)
XLA Modules:
  0.0 53.7 jit_solution(1327427430973273497)
XLA Ops:
  0.6 52.4 %gcn_step.1 = (bf16[128,128]{1,0:T(8,128)(2,1)S(1)}, f32[128,128]{1,0:T(8,128)S(1)}, f32[1,128]{1,0:T(1,128)S(1)}, bf16[128,128]{1,0:T(8,128)(2,1)S(1)}) custom-call(bf16[128,128]{1,0:T(8,128)(2,1)} %refs_0_.1, bf16[128,128]{1,0:T(8,128)(2,1)} %refs_1_.1, f32[1,128]{1,0:T(1,128)} %bitcast.4, bf16[1,5,28,128,128]{4,3,2,1,0:T(8,128)(2,1)} %refs_3_.1, ...), custom_call_target="tpu_custom_call" | custom-call | tf_op jit(solution)/shard_map/gcn_step/pallas_call | solution.py:280
  53.0 0.7 %finish.1 = (bf16[128,128]{1,0:T(8,128)(2,1)}, f32[128,128]{1,0:T(8,128)}, f32[1,128]{1,0:T(1,128)}, bf16[128,128]{1,0:T(8,128)(2,1)}) custom-call(bf16[128,128]{1,0:T(8,128)(2,1)S(1)} %get-tuple-element.12.hidden, f32[128,128]{1,0:T(8,128)S(1)} %get-tuple-element.13.gw, f32[1,128]{1,0:T(1,128)S(1)} %get-tuple-element.14.gb, ...), custom_call_target="tpu_custom_call" | custom-call | tf_op jit(solution)/shard_map/finish/pallas_call | solution.py:321

commit v4 on v3

--- a/solution.py
+++ b/solution.py
@@ -23,7 +23,7 @@
     hidden_o, gw_o, gb_o, gf_o,
     tl, adj, xbuf, pown, psib, qbuf, rsend, rbuf, zsend, zrecv, w_v, b_v, cot_v, cols_s, count_s,
     gsend, grecv, asend, arecv, whole_v, full_v,
-    lsem, xr, sibr, qr, pr, fzr, bzr, gr, ssem,
+    lsem, xr, sibr, qr, pr, fzr, bzr, half_r, gr, ssem,
 ):
     slots, max_tiles, block = tl.shape[0], tl.shape[1], tl.shape[2]
     chips = rep_size // 2
@@ -50,8 +50,12 @@
     barrier = pltpu.get_barrier_semaphore()
     for m in near:
         pl.semaphore_signal(barrier, inc=1, device_id=dpeer(m), device_id_type=MESH)
-    for q in range(plane_size - 1, 0, -1):
-        pl.semaphore_signal(barrier, inc=1, device_id=ppeer(q), device_id_type=MESH)
+    for j in [6, 7, 4, 5, 2, 3, 1]:
+        pl.semaphore_signal(barrier, inc=1, device_id=rpeer(j), device_id_type=MESH)
+    for q in range(1, y_size):
+        pl.semaphore_signal(barrier, inc=1, device_id=ppeer(q * rep_size), device_id_type=MESH)
+    wide = sorted(range(1, plane_size), key=lambda q: (-min(q // 8, 4 - q // 8) - min(q % 8 // 2, 4 - q % 8 // 2), -q))
+    deep = sorted(range(1, depth), key=lambda m: (-min(m, depth - m), m))
 
     loc = [
         pltpu.make_async_copy(feats, xbuf.at[0, 0, 0], lsem.at[0]),
@@ -111,9 +115,10 @@
 
     half = chips * block
 
-    def spread(k):
-        for i in range(1, chips):
-            go("X", xbuf.at[k, 0, 0], xbuf.at[k, 0, i], ssem.at[1], xr.at[k], rpeer(2 * i))
+    def spread(k, rows=slice(None)):
+        for i in (2, 1, 3):
+            src = feats if k == 0 else xbuf.at[k, 0, 0, rows]
+            go("X", src, xbuf.at[k, 0, i, rows], ssem.at[1], xr.at[k], rpeer(2 * i))
 
     def share(k):
         arrived("X", xbuf.at[k, 0, 1:], xr.at[k])
@@ -121,6 +126,8 @@
 
     def fetched(k):
         arrived("F", xbuf.at[k, 0, 0], fzr.at[k])
+
+    parts = [slice(0, block // 2), slice(block // 2, block)]
 
     def product(k, h):
         if h == 1:
@@ -129,10 +136,11 @@
             adj[k, :, h * half:(h + 1) * half], xbuf[k, h].reshape(half, block), preferred_element_type=F32
         )
 
-    loc[0].wait()
-    pl.semaphore_wait(barrier, len(near) + plane_size - 1)
-    for k in range(2, slots):
-        go("F", xbuf.at[0, 0, 0], xbuf.at[k, 0, 0], ssem.at[0], fzr.at[k], zpeer(k))
+    pl.semaphore_wait(barrier, len(near) + rep_size + y_size - 2)
+    for n, rows in enumerate(parts):
+        go("F", feats.at[rows], xbuf.at[2, 0, 0, rows], ssem.at[0], half_r.at[n], zpeer(2))
+    for k in range(3, slots):
+        go("F", feats, xbuf.at[k, 0, 0], ssem.at[0], fzr.at[k], zpeer(k))
     spread(0)
     for c in loc[1:]:
         c.wait()
@@ -141,10 +149,12 @@
     spread(4)
     fetched(3)
     spread(3)
+    loc[0].wait()
     share(0)
     build(4)
-    fetched(2)
-    go("F", xbuf.at[2, 0, 0], xbuf.at[1, 0, 0], ssem.at[0], fzr.at[1], dpeer(3 * depth // 4))
+    for n, rows in enumerate(parts):
+        arrived("F", xbuf.at[2, 0, 0, rows], half_r.at[n])
+        go("F", xbuf.at[2, 0, 0, rows], xbuf.at[1, 0, 0, rows], ssem.at[0], half_r.at[2 + n], dpeer(3 * depth // 4))
     spread(2)
     build(3)
     share(4)
@@ -156,8 +166,9 @@
     total = total + product(3, 0) + product(3, 1)
     for c in late:
         c.wait()
-    fetched(1)
-    spread(1)
+    for n, rows in enumerate(parts):
+        arrived("F", xbuf.at[1, 0, 0, rows], half_r.at[2 + n])
+        spread(1, rows)
     total = total + product(2, 0) + product(2, 1)
     share(1)
     total = total + product(1, 0)
@@ -183,7 +194,7 @@
         rows = gw[4 * p:4 * p + 8]
         gsend[p] = jnp.where(low, rows, gb).astype(BF16)
         gsend[p + 1] = jnp.where(low, gb, rows).astype(BF16)
-    for q in range(1, plane_size):
+    for q in wide:
         go("G", gsend.at[jnp.bitwise_xor(plane, q)], grecv.at[q], ssem.at[6], gr.at[0], ppeer(q))
 
     back = lax.dot_general(w, g, (((1,), (1,)), ((), ())), preferred_element_type=F32).astype(BF16)
@@ -220,7 +231,7 @@
     push(3)
     arrived("G", grecv.at[1:], gr.at[0])
     asend[...] = tree_sum([gsend[plane].astype(F32)] + [grecv[q].astype(F32) for q in range(1, plane_size)]).astype(BF16)
-    for m in range(1, depth):
+    for m in deep:
         go("G", asend, arecv.at[m], ssem.at[7], gr.at[1], dpeer(m))
     pair(2)
     push(4)
@@ -236,18 +247,19 @@
     hidden_o[...] = (v * cdf).astype(BF16)
     arrived("G", arecv.at[1:], gr.at[1])
     whole = tree_sum([asend[...].astype(F32)] + [arecv[m].astype(F32) for m in range(1, depth)])
-    whole_v[...] = whole
-    full_v[plane] = whole
-    for q in range(1, plane_size):
+    odd = (plane & 1) == 1
+    mine = jnp.where(odd, whole[4:8], whole[0:4])
+    whole_v[...] = mine
+    full_v[plane] = mine
+    for q in wide:
         go("G", whole_v, full_v.at[plane], ssem.at[8], gr.at[2], ppeer(q))
-    gb_o[...] = jnp.where((plane & 1) == 0, whole[4:5], whole[0:1])
+    gb_o[...] = jnp.where(odd, whole[0:1], whole[4:5])
     for k in range(slots - 1, 0, -1):
         arrived("Z", zrecv.at[k], bzr.at[k])
         acc = acc + zrecv[k].astype(F32)
     gf_o[...] = acc.T.astype(BF16)
     arrived("G", full_v.at[1:], gr.at[2])
-    for p in range(0, plane_size, 2):
-        gw_o[4 * p:4 * p + 8] = jnp.where(low, full_v[p], full_v[p + 1])
+    gw_o[...] = full_v[...].reshape(block, block)
     arrived("F", zsend.at[1:], ssem.at[0])
     arrived("X", rsend.at[:, 1:], ssem.at[1])
     arrived("X", psib, ssem.at[2])
@@ -307,11 +319,11 @@
                 vmem((y_size * rep_size, 8, block), BF16),
                 vmem((8, block), BF16),
                 vmem((dom_size // y_size, 8, block), BF16),
-                vmem((8, block), F32),
-                vmem((y_size * rep_size, 8, block), F32),
+                vmem((4, block), F32),
+                vmem((y_size * rep_size, 4, block), F32),
                 dma((6 + slots,)),
                 dma((slots,)), dma((slots,)), dma((slots,)), dma((slots,)), dma((slots,)), dma((slots,)),
-                dma((3,)), dma((9,)),
+                dma((4,)), dma((3,)), dma((9,)),
             ],
             compiler_params=pltpu.CompilerParams(
                 collective_id=0, has_side_effects=True

time: 53.8 us -> 50.2 us (0.933)
  Pallas kernels: 53 us -> 49.5 us
    pallas_call x1, Pallas kernels: 52.4 us -> 48.8 us  [body(): pl.pallas_call(lambda *refs: kernel(dom_size, rep_size, y_size, *refs), o...]
where the time goes in v4:
time: 50.2 us; the launch traced here: 50.1 us
  Pallas kernels  49.5 us (99%)
  between operations  0.64 us (1%)
    pallas_call x1, Pallas kernels, body(): pl.pallas_call(lambda *refs: kernel(dom_size, rep_size, y_size, *refs), o...  48.8 us

profile of v4, /device:TPU:1, one launch (start us, length us, event | category | flops | bytes accessed | tf_op | source)
XLA Modules:
  0.0 50.1 jit_solution(32243063582955038)
XLA Ops:
  0.6 48.8 %gcn_step.1 = (bf16[128,128]{1,0:T(8,128)(2,1)S(1)}, f32[128,128]{1,0:T(8,128)S(1)}, f32[1,128]{1,0:T(1,128)S(1)}, bf16[128,128]{1,0:T(8,128)(2,1)S(1)}) custom-call(bf16[128,128]{1,0:T(8,128)(2,1)} %refs_0_.1, bf16[128,128]{1,0:T(8,128)(2,1)} %refs_1_.1, f32[1,128]{1,0:T(1,128)} %bitcast.4, bf16[1,5,28,128,128]{4,3,2,1,0:T(8,128)(2,1)} %refs_3_.1, ...), custom_call_target="tpu_custom_call" | custom-call | tf_op jit(solution)/shard_map/gcn_step/pallas_call | solution.py:292
  49.4 0.7 %finish.1 = (bf16[128,128]{1,0:T(8,128)(2,1)}, f32[128,128]{1,0:T(8,128)}, f32[1,128]{1,0:T(1,128)}, bf16[128,128]{1,0:T(8,128)(2,1)}) custom-call(bf16[128,128]{1,0:T(8,128)(2,1)S(1)} %get-tuple-element.12.hidden, f32[128,128]{1,0:T(8,128)S(1)} %get-tuple-element.13.gw, f32[1,128]{1,0:T(1,128)S(1)} %get-tuple-element.14.gb, ...), custom_call_target="tpu_custom_call" | custom-call | tf_op jit(solution)/shard_map/finish/pallas_call | solution.py:333

commit v5 on v4

--- a/solution.py
+++ b/solution.py
@@ -9,6 +9,7 @@
 F32 = jnp.float32
 BF16 = jnp.bfloat16
 ROWS = 16
+CUTS = 2
 
 
 def tree_sum(parts):
@@ -23,7 +24,7 @@
     hidden_o, gw_o, gb_o, gf_o,
     tl, adj, xbuf, pown, psib, qbuf, rsend, rbuf, zsend, zrecv, w_v, b_v, cot_v, cols_s, count_s,
     gsend, grecv, asend, arecv, whole_v, full_v,
-    lsem, xr, sibr, qr, pr, fzr, bzr, half_r, gr, ssem,
+    lsem, xr, sibr, qr, pr, fzr, bzr, half_r, last_r, gr, ssem,
 ):
     slots, max_tiles, block = tl.shape[0], tl.shape[1], tl.shape[2]
     chips = rep_size // 2
@@ -115,10 +116,10 @@
 
     half = chips * block
 
-    def spread(k, rows=slice(None)):
+    def spread(k, rows=slice(None), sem=None):
         for i in (2, 1, 3):
             src = feats if k == 0 else xbuf.at[k, 0, 0, rows]
-            go("X", src, xbuf.at[k, 0, i, rows], ssem.at[1], xr.at[k], rpeer(2 * i))
+            go("X", src, xbuf.at[k, 0, i, rows], ssem.at[1], xr.at[k] if sem is None else sem, rpeer(2 * i))
 
     def share(k):
         arrived("X", xbuf.at[k, 0, 1:], xr.at[k])
@@ -127,7 +128,8 @@
     def fetched(k):
         arrived("F", xbuf.at[k, 0, 0], fzr.at[k])
 
-    parts = [slice(0, block // 2), slice(block // 2, block)]
+    step = block // CUTS
+    parts = [slice(n * step, (n + 1) * step) for n in range(CUTS)]
 
     def product(k, h):
         if h == 1:
@@ -154,7 +156,7 @@
     build(4)
     for n, rows in enumerate(parts):
         arrived("F", xbuf.at[2, 0, 0, rows], half_r.at[n])
-        go("F", xbuf.at[2, 0, 0, rows], xbuf.at[1, 0, 0, rows], ssem.at[0], half_r.at[2 + n], dpeer(3 * depth // 4))
+        go("F", xbuf.at[2, 0, 0, rows], xbuf.at[1, 0, 0, rows], ssem.at[0], half_r.at[CUTS + n], dpeer(3 * depth // 4))
     spread(2)
     build(3)
     share(4)
@@ -167,17 +169,21 @@
     for c in late:
         c.wait()
     for n, rows in enumerate(parts):
-        arrived("F", xbuf.at[1, 0, 0, rows], half_r.at[2 + n])
-        spread(1, rows)
+        arrived("F", xbuf.at[1, 0, 0, rows], half_r.at[CUTS + n])
+        spread(1, rows, last_r.at[2 * n // CUTS])
     total = total + product(2, 0) + product(2, 1)
-    share(1)
+    for n, rows in enumerate((slice(0, block // 2), slice(block // 2, block))):
+        arrived("X", xbuf.at[1, 0, 1:, rows], last_r.at[n])
+        go("X", xbuf.at[1, 0, :, rows], xbuf.at[1, 1, :, rows], ssem.at[2], sibr.at[1], sibling)
     total = total + product(1, 0)
     total = total + product(1, 1)
 
     t_hi = total.astype(BF16)
     t_lo = (total - t_hi.astype(F32)).astype(BF16)
     w = w_v[...]
-    v = jnp.dot(t_hi, w, preferred_element_type=F32) + jnp.dot(t_lo, w, preferred_element_type=F32) + b_v[...]
+    v = jnp.dot(
+        jnp.concatenate([t_hi, t_lo], axis=1), jnp.concatenate([w, w], axis=0), preferred_element_type=F32
+    ) + b_v[...]
     c0 = 0.7978845608028654
     th = jnp.tanh(c0 * (v + 0.044715 * (v * v * v)))
     cdf = 0.5 * (1.0 + th)
@@ -185,8 +191,11 @@
     grad_pre = cot_v[...].astype(F32) * deriv
     g = grad_pre.astype(BF16)
 
-    gw = lax.dot_general(t_hi, g, (((0,), (0,)), ((), ())), preferred_element_type=F32) + lax.dot_general(
-        t_lo, g, (((0,), (0,)), ((), ())), preferred_element_type=F32
+    gw = lax.dot_general(
+        jnp.concatenate([t_hi, t_lo], axis=0),
+        jnp.concatenate([g, g], axis=0),
+        (((0,), (0,)), ((), ())),
+        preferred_element_type=F32,
     )
     gb = jnp.broadcast_to(jnp.sum(grad_pre, axis=0, keepdims=True), (8, block))
     low = lax.broadcasted_iota(jnp.int32, (8, block), 0) < 4
@@ -242,9 +251,6 @@
     pair(0)
     cross(2)
     cross(3)
-    cross(4)
-    acc = gathered(0)
-    hidden_o[...] = (v * cdf).astype(BF16)
     arrived("G", arecv.at[1:], gr.at[1])
     whole = tree_sum([asend[...].astype(F32)] + [arecv[m].astype(F32) for m in range(1, depth)])
     odd = (plane & 1) == 1
@@ -254,6 +260,9 @@
     for q in wide:
         go("G", whole_v, full_v.at[plane], ssem.at[8], gr.at[2], ppeer(q))
     gb_o[...] = jnp.where(odd, whole[0:1], whole[4:5])
+    cross(4)
+    acc = gathered(0)
+    hidden_o[...] = (v * cdf).astype(BF16)
     for k in range(slots - 1, 0, -1):
         arrived("Z", zrecv.at[k], bzr.at[k])
         acc = acc + zrecv[k].astype(F32)
@@ -323,7 +332,7 @@
                 vmem((y_size * rep_size, 4, block), F32),
                 dma((6 + slots,)),
                 dma((slots,)), dma((slots,)), dma((slots,)), dma((slots,)), dma((slots,)), dma((slots,)),
-                dma((4,)), dma((3,)), dma((9,)),
+                dma((2 * CUTS,)), dma((2,)), dma((3,)), dma((9,)),
             ],
             compiler_params=pltpu.CompilerParams(
                 collective_id=0, has_side_effects=True

time: 50.2 us -> 50.1 us (level)
  no operation moved by 1% of the time
where the time goes in v5:
time: 50.1 us; the launch traced here: 50 us
  Pallas kernels  49.3 us (98%)
  between operations  0.64 us (1%)
    pallas_call x1, Pallas kernels, body(): pl.pallas_call(lambda *refs: kernel(dom_size, rep_size, y_size, *refs), o...  48.7 us

profile of v5, /device:TPU:1, one launch (start us, length us, event | category | flops | bytes accessed | tf_op | source)
XLA Modules:
  0.0 50.0 jit_solution(12065495971132413193)
XLA Ops:
  0.6 48.7 %gcn_step.1 = (bf16[128,128]{1,0:T(8,128)(2,1)S(1)}, f32[128,128]{1,0:T(8,128)S(1)}, f32[1,128]{1,0:T(1,128)S(1)}, bf16[128,128]{1,0:T(8,128)(2,1)S(1)}) custom-call(bf16[128,128]{1,0:T(8,128)(2,1)} %refs_0_.1, bf16[128,128]{1,0:T(8,128)(2,1)} %refs_1_.1, f32[1,128]{1,0:T(1,128)} %bitcast.4, bf16[1,5,28,128,128]{4,3,2,1,0:T(8,128)(2,1)} %refs_3_.1, ...), custom_call_target="tpu_custom_call" | custom-call | tf_op jit(solution)/shard_map/gcn_step/pallas_call | solution.py:301
  49.3 0.7 %finish.1 = (bf16[128,128]{1,0:T(8,128)(2,1)}, f32[128,128]{1,0:T(8,128)}, f32[1,128]{1,0:T(1,128)}, bf16[128,128]{1,0:T(8,128)(2,1)}) custom-call(bf16[128,128]{1,0:T(8,128)(2,1)S(1)} %get-tuple-element.12.hidden, f32[128,128]{1,0:T(8,128)S(1)} %get-tuple-element.13.gw, f32[1,128]{1,0:T(1,128)S(1)} %get-tuple-element.14.gb, ...), custom_call_target="tpu_custom_call" | custom-call | tf_op jit(solution)/shard_map/finish/pallas_call | solution.py:342
